TPU v7x, 32 devices: a whole 2x2x4 slice. The times are simulated.
32 devices in a mesh: blk: 16 (over z, y, x), feat: 2 (over core).
Axes of the slice: x: 2, y: 2, z: 4, core: 2. Of those that a mesh axis runs over, the one named last changes fastest.
Arguments:
- points: bfloat16 [16384, 64], P('blk', 'feat'), may hold values from -1.5 to 1.5
- vectors: bfloat16 [16384, 64], P('blk', 'feat'), may hold values from -5.5 to 5.5
- lengthscale: float32 [64], replicated, may hold values from 0.5 to 2
- outscale: float32 [1], replicated, may hold values from 0.1 to 0.4
- noise: float32 [1], replicated, may hold values from 0.05 to 0.5
Outputs:
- product: float32 [16384, 64], P('blk', 'feat')
All inputs are finite; a program needn't handle non-finite values.
Results may differ from a plain program's by a relative error of at most 0.0026.
Values may be sent and summed in bfloat16 or wider, within the bound.
A program may use at most 64 MiB of HBM per device.

v0:
```python
import functools

import jax
import jax.numpy as jnp
from jax import lax
from jax.experimental import pallas as pl
from jax.experimental.pallas import tpu as pltpu
from jax.sharding import PartitionSpec as P

LOG2E = 1.4426950408889634
F32 = jnp.float32
BF16 = jnp.bfloat16
EXTRA = 16
PLANE = 4


def pieces(value):
    first = value.astype(BF16).astype(F32)
    rest = value - first
    second = rest.astype(BF16).astype(F32)
    return first, second, rest - second


def extra_rows(rows):
    shape = (EXTRA, rows[0].shape[1])
    place = lax.broadcasted_iota(jnp.int32, shape, 0)
    out = jnp.zeros(shape, F32)
    for index, row in enumerate(rows):
        out = jnp.where(place == index, row, out)
    return out.astype(BF16)


def kernel(
    line, points, vectors, lengths_in, outscale_in, noise_in, result,
    lengths, outscale, noise, small_sem,
    columns, row_points, right, left, total, inbox, mine, swap_out, swap_in,
    local_sem, pair_send, pair_recv, plane_send, plane_recv, twin_send, twin_recv,
    row_send, row_recv, part_send, part_recv, swap_send, swap_recv,
):
    me = lax.axis_index("blk")
    core = lax.axis_index("feat")
    other = 1 - core
    half, rows = points.shape
    feats = 2 * half
    share = rows // 2

    def remote(src, dst, send, arrive, blk, feat):
        return pltpu.make_async_remote_copy(
            src_ref=src, dst_ref=dst, send_sem=send, recv_sem=arrive,
            device_id={"blk": blk, "feat": feat}, device_id_type=pl.DeviceIdType.MESH,
        )

    small = [
        pltpu.make_async_copy(lengths_in, lengths, small_sem.at[0]),
        pltpu.make_async_copy(outscale_in, outscale, small_sem.at[1]),
        pltpu.make_async_copy(noise_in, noise, small_sem.at[2]),
    ]
    for copy in small:
        copy.start()
    barrier = pltpu.get_barrier_semaphore()

    def greet(blk, feat):
        pl.semaphore_signal(
            barrier, inc=1, device_id={"blk": blk, "feat": feat},
            device_id_type=pl.DeviceIdType.MESH,
        )

    def column_peer(index):
        return me ^ ((index % 2) * 2 + (index // 2) * (2 * line))

    def row_peer(step):
        return me ^ (step % 2 + (step // 2) * PLANE)

    greet(me, other)
    greet(column_peer(1), core)
    greet(column_peer(2), core)
    for step in range(1, line):
        greet(row_peer(step), core)

    my_rows = pl.ds(pl.multiple_of(core * half, half), half)
    my_vector_rows = pl.ds(pl.multiple_of(feats + core * half, half), half)

    locals_ = []
    pair = []
    for part in range(2):
        cols = pl.ds(part * share, share)
        for place, (array, spot_rows) in enumerate(((points, my_rows), (vectors, my_vector_rows))):
            slot = 2 * part + place
            target = columns.at[0, part, spot_rows, :]
            locals_.append(
                pltpu.make_async_copy(array.at[:, cols], target, local_sem.at[slot]))
            pair.append(
                remote(array.at[:, cols], target, pair_send.at[slot], pair_recv.at[slot],
                       me, other))
    locals_.append(pltpu.make_async_copy(vectors, mine, local_sem.at[4]))
    for copy in locals_:
        copy.start()
    pl.semaphore_wait(barrier, 2 + line)
    for copy in pair:
        copy.start()

    for copy in small:
        copy.wait()
    scale = outscale[0]
    top = jnp.log(jnp.full((1, 1), scale, F32)) * LOG2E
    column = jnp.transpose(jnp.broadcast_to(lengths[...], (feats, feats)))[:, 0:1]

    for copy in locals_:
        copy.wait()
    for copy in pair:
        copy.wait_recv()

    def row_copy(step):
        return remote(columns.at[0, core, 0:feats, :], row_points.at[step],
                      row_send.at[step], row_recv.at[step], row_peer(step), core)

    def part_of(index, owner, piece):
        return columns.at[index, owner, pl.ds(piece * feats, feats), :]

    def column_copy(index, piece):
        source = 0 if index < 3 else 2
        return remote(part_of(source, core, piece), part_of(index, core, piece),
                      plane_send.at[index, piece], plane_recv.at[index, piece],
                      column_peer(1 if index == 3 else index), core)

    def start_row(step, carry):
        row_copy(step).start()
        return carry

    lax.fori_loop(1, line, start_row, 0)
    for piece in range(2):
        column_copy(1, piece).start()
        column_copy(2, piece).start()

    def twin(index, owner, piece):
        return remote(part_of(index, owner, piece), part_of(index, owner, piece),
                      twin_send.at[index, piece], twin_recv.at[index, piece], me, other)

    def fetch(index, piece):
        column_copy(index, piece).wait_recv()
        if index == 2:
            column_copy(3, piece).start()
        twin(index, core, piece).start()

    def prepare_columns(index):
        if index > 0:
            for piece in range(2):
                twin(index, other, piece).wait_recv()
        for part in range(2):
            guest = (columns[index, part, 0:feats, :].astype(F32) / column).astype(BF16)
            wide = guest.astype(F32)
            norm = -0.5 * LOG2E * jnp.sum(wide * wide, axis=0, keepdims=True)
            one = jnp.ones_like(norm)
            stacked = jnp.concatenate(
                [guest, guest, guest, extra_rows(pieces(norm) + (one, one, one))], axis=0)
            right[index, part * share:(part + 1) * share, :] = stacked.T

    def prepare_rows(step, value):
        scaled = (value.astype(F32) / column).astype(BF16).astype(F32)
        level = -0.5 * LOG2E * jnp.sum(scaled * scaled, axis=0, keepdims=True) + top
        one = jnp.ones_like(level)
        for index, piece in enumerate(pieces(scaled * LOG2E)):
            left[step, index * feats:(index + 1) * feats, :] = piece.astype(BF16)
        left[step, 3 * feats:, :] = extra_rows((one, one, one) + pieces(level))

    def unit(step, index, parts=(0, 1)):
        guests = slice(parts[0] * share, (parts[-1] + 1) * share)
        power = jnp.dot(right[index, guests, :], left[step], preferred_element_type=F32)
        value = jnp.exp2(jnp.minimum(power, top)).astype(BF16)
        for place, part in enumerate(parts):
            total[step] += jnp.dot(
                columns[index, part, feats:, :], value[place * share:(place + 1) * share],
                preferred_element_type=F32)

    def give_back(step):
        return remote(total.at[step], inbox.at[step], part_send.at[step],
                      part_recv.at[step], row_peer(step), core)

    total[...] = jnp.zeros_like(total)
    prepare_columns(0)
    for index in range(PLANE - 1):
        if index > 0:
            prepare_columns(index)

        def one_row(step, carry):
            if index == 0:
                @pl.when(step == 0)
                def _():
                    prepare_rows(step, columns[0, core, 0:feats, :])

                @pl.when(step > 0)
                def _():
                    row_copy(step).wait_recv()
                    prepare_rows(step, row_points[step])

            @pl.when(step == line - 2)
            def _():
                if index == 0:
                    fetch(1, 0)
                fetch(index + 1, 1)

            if index < PLANE - 2:
                @pl.when(step == line - 1)
                def _():
                    fetch(index + 2, 0)

            unit(step, index)
            return carry

        lax.fori_loop(0, line, one_row, 0)

    last = PLANE - 1
    prepare_columns(last)

    def last_row(place, carry):
        step = line - 1 - place
        unit(step, last)

        @pl.when(place > 0)
        def _():
            give_back(step + 1).start()
        return carry

    lax.fori_loop(0, line - 1, last_row, 0)
    unit(0, last, (0,))
    give_back(1).start()
    unit(0, last, (1,))

    def collect(place, carry):
        step = line - 1 - place
        give_back(step).wait_recv()
        total[0] += inbox[step]
        return carry

    lax.fori_loop(0, line - 1, collect, 0)

    other_rows = pl.ds(pl.multiple_of(other * half, half), half)
    swap_out[...] = total[0, other_rows, :]
    swap = remote(swap_out, swap_in, swap_send, swap_recv, me, other)
    factor = noise[0]
    my_cols = pl.ds(pl.multiple_of(core * share, share), share)
    other_cols = pl.ds(pl.multiple_of(other * share, share), share)
    result[:, my_cols] = total[0, my_rows, :] + factor * mine[:, my_cols].astype(F32)
    swap.start()
    swap.wait_recv()
    result[:, other_cols] = swap_in[...] + factor * mine[:, other_cols].astype(F32)

    swap.wait_send()
    for copy in pair:
        copy.wait_send()
    for index in range(1, PLANE):
        for piece in range(2):
            column_copy(index, piece).wait_send()
            twin(index, core, piece).wait_send()

    def drain(step, carry):
        give_back(step).wait_send()
        row_copy(step).wait_send()
        return carry

    lax.fori_loop(1, line, drain, 0)


def per_device(blk, points, vectors, lengthscale, outscale, noise):
    assert blk % (2 * PLANE) == 0 and blk & (blk - 1) == 0
    line = blk // PLANE
    rows, half = points.shape
    feats = 2 * half
    share = rows // 2
    vmem = pl.BlockSpec(memory_space=pltpu.VMEM)
    stay = pl.BlockSpec(memory_space=pltpu.HBM)
    dma = pltpu.SemaphoreType.DMA
    wide = 3 * feats + EXTRA
    out = pl.pallas_call(
        functools.partial(kernel, line),
        out_shape=jax.ShapeDtypeStruct((half, rows), F32),
        in_specs=[stay] * 5,
        out_specs=vmem,
        scratch_shapes=[
            pltpu.VMEM((1, feats), F32),
            pltpu.SMEM((1,), F32),
            pltpu.SMEM((1,), F32),
            dma((3,)),
            pltpu.VMEM((PLANE, 2, 2 * feats, share), BF16),
            pltpu.VMEM((line, feats, share), BF16),
            pltpu.VMEM((PLANE, rows, wide), BF16),
            pltpu.VMEM((line, wide, share), BF16),
            pltpu.VMEM((line, feats, share), F32),
            pltpu.VMEM((line, feats, share), F32),
            pltpu.VMEM((half, rows), BF16),
            pltpu.VMEM((half, share), F32),
            pltpu.VMEM((half, share), F32),
            dma((5,)),
            dma((4,)),
            dma((4,)),
            dma((PLANE, 2)),
            dma((PLANE, 2)),
            dma((PLANE, 2)),
            dma((PLANE, 2)),
            dma((line,)),
            dma((line,)),
            dma((line,)),
            dma((line,)),
            dma,
            dma,
        ],
        compiler_params=pltpu.CompilerParams(collective_id=0, has_side_effects=True),
        name="tile_solve",
    )(points.T, vectors.T, lengthscale.reshape(1, feats), outscale, noise)
    return out.T


def solution(mesh):
    placed = (P("blk", "feat"), P("blk", "feat"), P(), P(), P())
    return jax.shard_map(
        functools.partial(per_device, mesh.shape["blk"]),
        mesh=mesh, in_specs=placed, out_specs=P("blk", "feat"), check_vma=False,
    )
```

profile of v0, /device:TPU:9, one launch (start us, length us, event | category | flops | bytes accessed | tf_op | source)
XLA Modules:
  0.0 34.0 jit_solution(2064324025848743365)
XLA Ops:
  1.3 31.1 %tile_solve.1 = f32[32,1024]{1,0:T(8,128)} custom-call(bf16[32,1024]{1,0:T(8,128)(2,1)} %bitcast.5, bf16[32,1024]{1,0:T(8,128)(2,1)} %bitcast.6, f32[1,64]{1,0:T(1,128)} %bitcast.7, f32[1]{0:T(128)S(6)} %copy.7.outscale_in, f32[1]{0:T(128)S(6)} %copy.8.noise_in), custom_call_target="tpu_custom_call" | custom-call | tf_op jit(solution)/shard_map/tile_solve/pallas_call | solution.py:274
  32.4 1.6 %copy.9 = f32[1024,32]{0,1:T(8,128)} copy(f32[1024,32]{0,1:T(8,128)} %bitcast.4) | data formatting | bytes 262144
where the time goes:
time: 34.1 us; the launch traced here: 34 us
  Pallas kernels  31.1 us (91%)
  local copies, waits for them, and re-layouts  1.57 us (5%)
  between operations  1.3 us (4%)
    pallas_call x1, Pallas kernels, per_device(): pl.pallas_call(functools.partial(kernel, line), out_shape=jax.ShapeDtypeS...  31.1 us
    unnamed x1, local copies, waits for them, and re-layouts  1.57 us

commit v1 on v0

v1 whole, which is shorter than its diff:
```python
import functools

import jax
import jax.numpy as jnp
from jax import lax
from jax.experimental import pallas as pl
from jax.experimental.pallas import tpu as pltpu
from jax.sharding import PartitionSpec as P

LOG2E = 1.4426950408889634
F32 = jnp.float32
BF16 = jnp.bfloat16
EXTRA = 16
PLANE = 4


def pieces(value):
    first = value.astype(BF16).astype(F32)
    rest = value - first
    second = rest.astype(BF16).astype(F32)
    return first, second, rest - second


def extra_rows(rows):
    shape = (EXTRA, rows[0].shape[1])
    place = lax.broadcasted_iota(jnp.int32, shape, 0)
    out = jnp.zeros(shape, F32)
    for index, row in enumerate(rows):
        out = jnp.where(place == index, row, out)
    return out.astype(BF16)


def kernel(
    line, points, vectors, lengths_in, outscale_in, noise_in, result,
    lengths, outscale, noise, small_sem,
    columns, row_points, right, left, total, part_out, inbox, mine, swap_out, swap_in,
    twin_alive, plane_alive, line_alive,
    local_sem, pair_send, pair_recv, plane_send, plane_recv, twin_send, twin_recv,
    row_send, row_recv, part_send, part_recv, swap_send, swap_recv,
):
    me = lax.axis_index("blk")
    core = lax.axis_index("feat")
    other = 1 - core
    half, rows = points.shape
    feats = 2 * half
    share = rows // 2
    spot = me % PLANE
    level = me // PLANE

    def remote(src, dst, send, arrive, blk, feat):
        return pltpu.make_async_remote_copy(
            src_ref=src, dst_ref=dst, send_sem=send, recv_sem=arrive,
            device_id={"blk": blk, "feat": feat}, device_id_type=pl.DeviceIdType.MESH,
        )

    def signal(sem, blk, feat):
        pl.semaphore_signal(
            sem, inc=1, device_id={"blk": blk, "feat": feat},
            device_id_type=pl.DeviceIdType.MESH,
        )

    def plane_peer(index):
        return me ^ index

    def line_peer(step):
        return me ^ (step * PLANE)

    def loop(first, last, body):
        def one(index, carry):
            body(index)
            return carry
        lax.fori_loop(first, last, one, 0)

    small = [
        pltpu.make_async_copy(lengths_in, lengths, small_sem.at[0]),
        pltpu.make_async_copy(outscale_in, outscale, small_sem.at[1]),
        pltpu.make_async_copy(noise_in, noise, small_sem.at[2]),
    ]
    my_rows = pl.ds(pl.multiple_of(core * half, half), half)
    other_rows = pl.ds(pl.multiple_of(other * half, half), half)
    my_cols = pl.ds(pl.multiple_of(core * share, share), share)
    other_cols = pl.ds(pl.multiple_of(other * share, share), share)
    inputs = (points, vectors)
    locals_ = [
        pltpu.make_async_copy(array, columns.at[0, kind, my_rows, :], local_sem.at[kind])
        for kind, array in enumerate(inputs)
    ]
    locals_.append(pltpu.make_async_copy(vectors, mine, local_sem.at[2]))
    for copy in small + locals_:
        copy.start()

    barrier = pltpu.get_barrier_semaphore()

    @pl.when(core == 0)
    def _():
        signal(barrier, me, other)

    for index in range(1, PLANE):
        @pl.when(plane_peer(index) > me)
        def _():
            signal(barrier, plane_peer(index), core)

    def greet_line(step):
        @pl.when(line_peer(step) > me)
        def _():
            for feat in range(2):
                signal(barrier, line_peer(step), feat)

    loop(1, line, greet_line)
    before = core + spot + 2 * level

    @pl.when(before > 0)
    def _():
        pl.semaphore_wait(barrier, before)

    @pl.when(core == 1)
    def _():
        signal(twin_alive, me, other)

    for index in range(1, PLANE):
        @pl.when(plane_peer(index) < me)
        def _():
            signal(plane_alive.at[index], plane_peer(index), core)

    def answer_line(step):
        @pl.when(line_peer(step) < me)
        def _():
            for feat in range(2):
                signal(line_alive.at[step, core], line_peer(step), feat)

    loop(1, line, answer_line)

    pair = [
        remote(array, columns.at[0, kind, my_rows, :], pair_send.at[kind], pair_recv.at[kind],
               me, other)
        for kind, array in enumerate(inputs)
    ]

    def plane_copy(index, kind):
        return remote(inputs[kind], columns.at[index, kind, my_rows, :],
                      plane_send.at[index, kind], plane_recv.at[index, kind],
                      plane_peer(index), core)

    def twin(index, kind):
        place = columns.at[index, kind, my_rows, :]
        return remote(place, place, twin_send.at[index, kind], twin_recv.at[index, kind],
                      me, other)

    def row_copy(step, feat):
        return remote(points.at[:, feat * share:(feat + 1) * share],
                      row_points.at[step, my_rows, :],
                      row_send.at[step, feat], row_recv.at[step, core],
                      line_peer(step), feat)

    def row_arrival(step, feat):
        spots = pl.ds(feat * half, half)
        return remote(points.at[:, 0:share], row_points.at[step, spots, :],
                      row_send.at[step, feat], row_recv.at[step, feat],
                      line_peer(step), feat)

    def send_plane(index):
        for kind in range(2):
            plane_copy(index, kind).start()

    for index in range(1, PLANE):
        @pl.when(plane_peer(index) < me)
        def _():
            send_plane(index)

    def send_low(step):
        @pl.when(line_peer(step) < me)
        def _():
            for feat in range(2):
                row_copy(step, feat).start()

    loop(1, line, send_low)

    @pl.when(core == 0)
    def _():
        pl.semaphore_wait(twin_alive, 1)

    for copy in pair:
        copy.start()

    for index in range(1, PLANE):
        @pl.when(plane_peer(index) > me)
        def _():
            pl.semaphore_wait(plane_alive.at[index], 1)
            send_plane(index)

    def send_high(step):
        @pl.when(line_peer(step) > me)
        def _():
            for feat in range(2):
                pl.semaphore_wait(line_alive.at[step, feat], 1)
                row_copy(step, feat).start()

    for copy in small:
        copy.wait()
    scale = outscale[0]
    top = jnp.log(jnp.full((1, 1), scale, F32)) * LOG2E
    column = jnp.transpose(jnp.broadcast_to(lengths[...], (feats, feats)))[:, 0:1]

    for copy in locals_:
        copy.wait()
    for copy in pair:
        copy.wait_recv()

    def prepare_columns(index):
        for part in range(2):
            cols = slice(part * share, (part + 1) * share)
            guest = (columns[index, 0, :, cols].astype(F32) / column).astype(BF16)
            wide = guest.astype(F32)
            norm = -0.5 * LOG2E * jnp.sum(wide * wide, axis=0, keepdims=True)
            one = jnp.ones_like(norm)
            stacked = jnp.concatenate(
                [guest, guest, guest, extra_rows(pieces(norm) + (one, one, one))], axis=0)
            right[index, cols, :] = stacked.T

    def prepare_rows(step, value):
        scaled = (value.astype(F32) / column).astype(BF16).astype(F32)
        height = -0.5 * LOG2E * jnp.sum(scaled * scaled, axis=0, keepdims=True) + top
        one = jnp.ones_like(height)
        for index, piece in enumerate(pieces(scaled * LOG2E)):
            left[step, index * feats:(index + 1) * feats, :] = piece.astype(BF16)
        left[step, 3 * feats:, :] = extra_rows((one, one, one) + pieces(height))

    def unit(step, index):
        power = jnp.dot(right[index], left[step], preferred_element_type=F32)
        value = jnp.exp2(jnp.minimum(power, top)).astype(BF16)
        return jnp.dot(columns[index, 1], value, preferred_element_type=F32)

    def give_back(step, feat):
        return remote(part_out.at[step, feat], inbox.at[step, core],
                      part_send.at[step, feat], part_recv.at[step, core],
                      line_peer(step), feat)

    def back_arrival(step, feat):
        return remote(part_out.at[step, feat], inbox.at[step, feat],
                      part_send.at[step, feat], part_recv.at[step, feat],
                      line_peer(step), feat)

    def forward(index):
        for kind in range(2):
            plane_copy(index, kind).wait_recv()
            twin(index, kind).start()

    prepare_columns(0)

    def first(step):
        @pl.when(step == 0)
        def _():
            prepare_rows(step, columns[0, 0, :, my_cols])

        @pl.when(step == 1)
        def _():
            loop(1, line, send_high)
            forward(1)
            forward(2)

        @pl.when(step == 2)
        def _():
            forward(3)

        @pl.when(step > 0)
        def _():
            for feat in range(2):
                row_arrival(step, feat).wait_recv()
            prepare_rows(step, row_points[step])

        total[step] = unit(step, 0)

    loop(0, line, first)

    def rest(place):
        step = jnp.where(
            place < line - 1, level ^ (place + jnp.where(place >= level, 1, 0)), 0)

        def one_column(index):
            @pl.when(place == 0)
            def _():
                for kind in range(2):
                    twin(index, kind).wait_recv()
                prepare_columns(index)

            total[step] += unit(step, index)

        loop(1, PLANE, one_column)

        @pl.when(place < line - 1)
        def _():
            for feat in range(2):
                part_out[step, feat] = (
                    total[step, feat * half:(feat + 1) * half, :].astype(BF16))
            for feat in range(2):
                give_back(step, feat).start()

    loop(0, line, rest)

    swap_out[...] = total[0, other_rows, :]
    swap = remote(swap_out, swap_in, swap_send, swap_recv, me, other)
    swap.start()
    factor = noise[0]
    result[:, my_cols] = total[0, my_rows, :] + factor * mine[:, my_cols].astype(F32)
    result[:, other_cols] = factor * mine[:, other_cols].astype(F32)

    def collect(step):
        for feat in range(2):
            back_arrival(step, feat).wait_recv()
            result[:, feat * share:(feat + 1) * share] += inbox[step, feat].astype(F32)

    loop(1, line, collect)
    swap.wait_recv()
    result[:, other_cols] += swap_in[...]

    swap.wait_send()
    for copy in pair:
        copy.wait_send()
    for index in range(1, PLANE):
        for kind in range(2):
            plane_copy(index, kind).wait_send()
            twin(index, kind).wait_send()

    def drain(step):
        for feat in range(2):
            give_back(step, feat).wait_send()
            row_copy(step, feat).wait_send()

    loop(1, line, drain)


def per_device(blk, points, vectors, lengthscale, outscale, noise):
    assert blk % (4 * PLANE) == 0 and blk & (blk - 1) == 0
    line = blk // PLANE
    rows, half = points.shape
    feats = 2 * half
    share = rows // 2
    stay = pl.BlockSpec(memory_space=pltpu.HBM)
    vmem = pl.BlockSpec(memory_space=pltpu.VMEM)
    dma = pltpu.SemaphoreType.DMA
    regular = pltpu.SemaphoreType.REGULAR
    wide = 3 * feats + EXTRA
    out = pl.pallas_call(
        functools.partial(kernel, line),
        out_shape=pltpu.VMEM((half, rows), F32),
        in_specs=[stay] * 5,
        out_specs=vmem,
        scratch_shapes=[
            pltpu.VMEM((1, feats), F32),
            pltpu.SMEM((1,), F32),
            pltpu.SMEM((1,), F32),
            dma((3,)),
            pltpu.VMEM((PLANE, 2, feats, rows), BF16),
            pltpu.VMEM((line, feats, share), BF16),
            pltpu.VMEM((PLANE, rows, wide), BF16),
            pltpu.VMEM((line, wide, share), BF16),
            pltpu.VMEM((line, feats, share), F32),
            pltpu.VMEM((line, 2, half, share), BF16),
            pltpu.VMEM((line, 2, half, share), BF16),
            pltpu.VMEM((half, rows), BF16),
            pltpu.VMEM((half, share), F32),
            pltpu.VMEM((half, share), F32),
            regular,
            regular((PLANE,)),
            regular((line, 2)),
            dma((3,)),
            dma((2,)),
            dma((2,)),
            dma((PLANE, 2)),
            dma((PLANE, 2)),
            dma((PLANE, 2)),
            dma((PLANE, 2)),
            dma((line, 2)),
            dma((line, 2)),
            dma((line, 2)),
            dma((line, 2)),
            dma,
            dma,
        ],
        compiler_params=pltpu.CompilerParams(collective_id=0, has_side_effects=True),
        name="tile_solve",
    )(points.T, vectors.T, lengthscale.reshape(1, feats), outscale, noise)
    return out.T


def solution(mesh):
    placed = (P("blk", "feat"), P("blk", "feat"), P(), P(), P())
    return jax.shard_map(
        functools.partial(per_device, mesh.shape["blk"]),
        mesh=mesh, in_specs=placed, out_specs=P("blk", "feat"), check_vma=False,
    )
```

time: 34.1 us -> 25.8 us (0.76)
  the two profiles are of different devices: /device:TPU:9 before, /device:TPU:1 now
where the time goes in v1:
time: 25.8 us; the launch traced here: 25.7 us
  Pallas kernels  23.7 us (92%)
  between operations  1.3 us (5%)
  local copies, waits for them, and re-layouts  0.66 us (3%)
    pallas_call x1, Pallas kernels, per_device(): pl.pallas_call(functools.partial(kernel, line), out_shape=pltpu.VMEM((hal...  23.7 us
    unnamed x1, local copies, waits for them, and re-layouts  0.66 us

profile of v1, /device:TPU:1, one launch (start us, length us, event | category | flops | bytes accessed | tf_op | source)
XLA Modules:
  0.0 25.7 jit_solution(13045485990086871683)
XLA Ops:
  1.3 23.7 %tile_solve.1 = f32[32,1024]{1,0:T(8,128)S(1)} custom-call(bf16[32,1024]{1,0:T(8,128)(2,1)} %bitcast.5, bf16[32,1024]{1,0:T(8,128)(2,1)} %bitcast.6, f32[1,64]{1,0:T(1,128)} %bitcast.7, f32[1]{0:T(128)S(6)} %copy.8.outscale_in, f32[1]{0:T(128)S(6)} %copy.9.noise_in), custom_call_target="tpu_custom_call" | custom-call | tf_op jit(solution)/shard_map/tile_solve/pallas_call | solution.py:343
  25.0 0.7 %copy.7 = f32[1024,32]{0,1:T(8,128)} copy(f32[1024,32]{0,1:T(8,128)S(1)} %bitcast.4) | data formatting | bytes 262144

commit v2 on v1

--- a/solution.py
+++ b/solution.py
@@ -89,6 +89,16 @@
     for copy in small + locals_:
         copy.start()
 
+    def greets(index):
+        if index == 3:
+            return spot == 0
+        return plane_peer(index) > me
+
+    def answers(index):
+        if index == 3:
+            return spot == 3
+        return plane_peer(index) < me
+
     barrier = pltpu.get_barrier_semaphore()
 
     @pl.when(core == 0)
@@ -96,7 +106,7 @@
         signal(barrier, me, other)
 
     for index in range(1, PLANE):
-        @pl.when(plane_peer(index) > me)
+        @pl.when(greets(index))
         def _():
             signal(barrier, plane_peer(index), core)
 
@@ -107,7 +117,7 @@
                 signal(barrier, line_peer(step), feat)
 
     loop(1, line, greet_line)
-    before = core + spot + 2 * level
+    before = core + jnp.where(spot == 3, 3, jnp.minimum(spot, 1)) + 2 * level
 
     @pl.when(before > 0)
     def _():
@@ -118,7 +128,7 @@
         signal(twin_alive, me, other)
 
     for index in range(1, PLANE):
-        @pl.when(plane_peer(index) < me)
+        @pl.when(answers(index))
         def _():
             signal(plane_alive.at[index], plane_peer(index), core)
 
@@ -147,14 +157,14 @@
                       me, other)
 
     def row_copy(step, feat):
-        return remote(points.at[:, feat * share:(feat + 1) * share],
+        return remote(columns.at[0, 0, my_rows, feat * share:(feat + 1) * share],
                       row_points.at[step, my_rows, :],
                       row_send.at[step, feat], row_recv.at[step, core],
                       line_peer(step), feat)
 
     def row_arrival(step, feat):
         spots = pl.ds(feat * half, half)
-        return remote(points.at[:, 0:share], row_points.at[step, spots, :],
+        return remote(columns.at[0, 0, my_rows, 0:share], row_points.at[step, spots, :],
                       row_send.at[step, feat], row_recv.at[step, feat],
                       line_peer(step), feat)
 
@@ -163,7 +173,7 @@
             plane_copy(index, kind).start()
 
     for index in range(1, PLANE):
-        @pl.when(plane_peer(index) < me)
+        @pl.when(answers(index))
         def _():
             send_plane(index)
 
@@ -173,6 +183,8 @@
             for feat in range(2):
                 row_copy(step, feat).start()
 
+    for copy in locals_:
+        copy.wait()
     loop(1, line, send_low)
 
     @pl.when(core == 0)
@@ -183,10 +195,14 @@
         copy.start()
 
     for index in range(1, PLANE):
-        @pl.when(plane_peer(index) > me)
+        @pl.when(greets(index))
         def _():
             pl.semaphore_wait(plane_alive.at[index], 1)
             send_plane(index)
+
+    @pl.when((spot == 1) | (spot == 2))
+    def _():
+        send_plane(3)
 
     def send_high(step):
         @pl.when(line_peer(step) > me)
@@ -201,8 +217,6 @@
     top = jnp.log(jnp.full((1, 1), scale, F32)) * LOG2E
     column = jnp.transpose(jnp.broadcast_to(lengths[...], (feats, feats)))[:, 0:1]
 
-    for copy in locals_:
-        copy.wait()
     for copy in pair:
         copy.wait_recv()
 
@@ -247,6 +261,11 @@
 
     prepare_columns(0)
 
+    def open_row(step):
+        for feat in range(2):
+            row_arrival(step, feat).wait_recv()
+        prepare_rows(step, row_points[step])
+
     def first(step):
         @pl.when(step == 0)
         def _():
@@ -255,45 +274,59 @@
         @pl.when(step == 1)
         def _():
             loop(1, line, send_high)
-            forward(1)
+            open_row(step)
+
+        total[step] = unit(step, 0)
+
+    loop(0, 2, first)
+    forward(1)
+
+    def upward(place):
+        return level ^ (place + jnp.where(place >= level, 1, 0))
+
+    def open_column(index):
+        for kind in range(2):
+            twin(index, kind).wait_recv()
+        prepare_columns(index)
+
+    def add_unit(step, index):
+        total[step] += unit(step, index)
+
+    def send_back(step):
+        for feat in range(2):
+            part_out[step, feat] = (
+                total[step, feat * half:(feat + 1) * half, :].astype(BF16))
+        for feat in range(2):
+            give_back(step, feat).start()
+
+    def rest(place):
+        step = jnp.where(place < line - 1, upward(place), 0)
+
+        @pl.when(step > 1)
+        def _():
+            open_row(step)
+            total[step] = unit(step, 0)
+
+        @pl.when(place == 0)
+        def _():
             forward(2)
-
-        @pl.when(step == 2)
-        def _():
-            forward(3)
-
-        @pl.when(step > 0)
-        def _():
-            for feat in range(2):
-                row_arrival(step, feat).wait_recv()
-            prepare_rows(step, row_points[step])
-
-        total[step] = unit(step, 0)
-
-    loop(0, line, first)
-
-    def rest(place):
-        step = jnp.where(
-            place < line - 1, level ^ (place + jnp.where(place >= level, 1, 0)), 0)
 
         def one_column(index):
             @pl.when(place == 0)
             def _():
-                for kind in range(2):
-                    twin(index, kind).wait_recv()
-                prepare_columns(index)
-
-            total[step] += unit(step, index)
+                open_column(index)
+
+            add_unit(step, index)
+
+            @pl.when((place == 0) & (index == 1))
+            def _():
+                forward(PLANE - 1)
 
         loop(1, PLANE, one_column)
 
         @pl.when(place < line - 1)
         def _():
-            for feat in range(2):
-                part_out[step, feat] = (
-                    total[step, feat * half:(feat + 1) * half, :].astype(BF16))
-            for feat in range(2):
-                give_back(step, feat).start()
+            send_back(step)
 
     loop(0, line, rest)
 
@@ -304,16 +337,6 @@
     result[:, my_cols] = total[0, my_rows, :] + factor * mine[:, my_cols].astype(F32)
     result[:, other_cols] = factor * mine[:, other_cols].astype(F32)
 
-    def collect(step):
-        for feat in range(2):
-            back_arrival(step, feat).wait_recv()
-            result[:, feat * share:(feat + 1) * share] += inbox[step, feat].astype(F32)
-
-    loop(1, line, collect)
-    swap.wait_recv()
-    result[:, other_cols] += swap_in[...]
-
-    swap.wait_send()
     for copy in pair:
         copy.wait_send()
     for index in range(1, PLANE):
@@ -327,6 +350,17 @@
             row_copy(step, feat).wait_send()
 
     loop(1, line, drain)
+
+    def collect(step):
+        for feat in range(2):
+            back_arrival(step, feat).wait_recv()
+            result[:, feat * share:(feat + 1) * share] += inbox[step, feat].astype(F32)
+
+    loop(1, line, collect)
+    swap.wait_recv()
+    result[:, other_cols] += swap_in[...]
+
+    swap.wait_send()
 
 
 def per_device(blk, points, vectors, lengthscale, outscale, noise):

time: 25.8 us -> 24.9 us (0.965)
  the two profiles are of different devices: /device:TPU:1 before, /device:TPU:27 now
where the time goes in v2:
time: 24.9 us; the launch traced here: 24.7 us
  Pallas kernels  22.7 us (91%)
  between operations  1.3 us (5%)
  local copies, waits for them, and re-layouts  0.66 us (3%)
    pallas_call x1, Pallas kernels, per_device(): pl.pallas_call(functools.partial(kernel, line), out_shape=pltpu.VMEM((hal...  22.7 us
    unnamed x1, local copies, waits for them, and re-layouts  0.66 us

profile of v2, /device:TPU:27, one launch (start us, length us, event | category | flops | bytes accessed | tf_op | source)
XLA Modules:
  0.0 24.7 jit_solution(9954988584767055100)
XLA Ops:
  1.3 22.7 %tile_solve.1 = f32[32,1024]{1,0:T(8,128)S(1)} custom-call(bf16[32,1024]{1,0:T(8,128)(2,1)} %bitcast.5, bf16[32,1024]{1,0:T(8,128)(2,1)} %bitcast.6, f32[1,64]{1,0:T(1,128)} %bitcast.7, f32[1]{0:T(128)S(6)} %copy.8.outscale_in, f32[1]{0:T(128)S(6)} %copy.9.noise_in), custom_call_target="tpu_custom_call" | custom-call | tf_op jit(solution)/shard_map/tile_solve/pallas_call | solution.py:377
  24.1 0.7 %copy.7 = f32[1024,32]{0,1:T(8,128)} copy(f32[1024,32]{0,1:T(8,128)S(1)} %bitcast.4) | data formatting | bytes 262144

commit v3 on v2

v3 whole, which is shorter than its diff:
```python
import functools

import jax
import jax.numpy as jnp
from jax import lax
from jax.experimental import pallas as pl
from jax.experimental.pallas import tpu as pltpu
from jax.sharding import PartitionSpec as P

LOG2E = 1.4426950408889634
F32 = jnp.float32
BF16 = jnp.bfloat16
EXTRA = 16
PLANE = 4


def pieces(value):
    first = value.astype(BF16).astype(F32)
    rest = value - first
    second = rest.astype(BF16).astype(F32)
    return first, second, rest - second


def extra_rows(rows):
    shape = (EXTRA, rows[0].shape[1])
    place = lax.broadcasted_iota(jnp.int32, shape, 0)
    out = jnp.zeros(shape, F32)
    for index, row in enumerate(rows):
        out = jnp.where(place == index, row, out)
    return out.astype(BF16)


def kernel(
    line, points, vectors, lengths_in, outscale, noise, result,
    lengths, columns, row_points, right, left, total, part_out, inbox, swap_out, swap_in,
    twin_alive, plane_alive, line_alive,
    small_sem, local_sem, plane_send, pair_recv, plane_recv, twin_send, twin_recv,
    row_send, row_recv, part_send, part_recv, swap_send, swap_recv,
):
    me = lax.axis_index("blk")
    core = lax.axis_index("feat")
    other = 1 - core
    half, rows = points.shape
    feats = 2 * half
    share = rows // 2
    spot = me % PLANE
    level = me // PLANE

    def remote(src, dst, send, arrive, blk, feat):
        return pltpu.make_async_remote_copy(
            src_ref=src, dst_ref=dst, send_sem=send, recv_sem=arrive,
            device_id={"blk": blk, "feat": feat}, device_id_type=pl.DeviceIdType.MESH,
        )

    def signal(sem, blk, feat):
        pl.semaphore_signal(
            sem, inc=1, device_id={"blk": blk, "feat": feat},
            device_id_type=pl.DeviceIdType.MESH,
        )

    def plane_peer(index):
        return me ^ index

    def line_peer(step):
        return me ^ (step * PLANE)

    def loop(first, last, body):
        def one(index, carry):
            body(index)
            return carry
        lax.fori_loop(first, last, one, 0)

    my_rows = pl.ds(pl.multiple_of(core * half, half), half)
    other_rows = pl.ds(pl.multiple_of(other * half, half), half)
    my_cols = pl.ds(pl.multiple_of(core * share, share), share)
    other_cols = pl.ds(pl.multiple_of(other * share, share), share)
    inputs = (points, vectors)
    small = pltpu.make_async_copy(lengths_in, lengths, small_sem)
    small.start()
    for kind, array in enumerate(inputs):
        pltpu.make_async_copy(array, columns.at[0, kind, my_rows, :], local_sem).start()

    def greets(index):
        if index == 3:
            return spot == 0
        return plane_peer(index) > me

    def answers(index):
        if index == 3:
            return spot == 3
        return plane_peer(index) < me

    barrier = pltpu.get_barrier_semaphore()

    @pl.when(core == 0)
    def _():
        signal(barrier, me, other)

    for index in range(1, PLANE):
        @pl.when(greets(index))
        def _():
            signal(barrier, plane_peer(index), core)

    def greet_line(step):
        @pl.when(line_peer(step) > me)
        def _():
            for feat in range(2):
                signal(barrier, line_peer(step), feat)

    loop(1, line, greet_line)
    before = core + jnp.where(spot == 3, 3, jnp.minimum(spot, 1)) + 2 * level

    @pl.when(before > 0)
    def _():
        pl.semaphore_wait(barrier, before)

    @pl.when(core == 1)
    def _():
        signal(twin_alive, me, other)

    for index in range(1, PLANE):
        @pl.when(answers(index))
        def _():
            signal(plane_alive.at[index - 1], plane_peer(index), core)

    def answer_line(step):
        @pl.when(line_peer(step) < me)
        def _():
            for feat in range(2):
                signal(line_alive.at[step - 1], line_peer(step), feat)

    loop(1, line, answer_line)

    def half_of(index):
        return columns.at[index, :, my_rows, :]

    def send_plane(index):
        for kind, array in enumerate(inputs):
            remote(array, columns.at[index, kind, my_rows, :], plane_send,
                   plane_recv.at[index - 1], plane_peer(index), core).start()

    def plane_arrival(index):
        return remote(half_of(index), half_of(index), plane_send, plane_recv.at[index - 1],
                      plane_peer(index), core)

    def twin(index):
        return remote(half_of(index), half_of(index), twin_send, twin_recv.at[index - 1],
                      me, other)

    def send_row(step):
        for feat in range(2):
            remote(columns.at[0, 0, my_rows, feat * share:(feat + 1) * share],
                   row_points.at[step, my_rows, :], row_send, row_recv.at[step - 1],
                   line_peer(step), feat).start()

    def row_arrival(step):
        return remote(row_points.at[step], row_points.at[step], row_send,
                      row_recv.at[step - 1], line_peer(step), core)

    for index in range(1, PLANE):
        @pl.when(answers(index))
        def _():
            send_plane(index)

    def send_low(step):
        @pl.when(line_peer(step) < me)
        def _():
            send_row(step)

    pltpu.make_async_copy(half_of(0), half_of(0), local_sem).wait()
    loop(1, line, send_low)

    @pl.when(core == 0)
    def _():
        pl.semaphore_wait(twin_alive, 1)

    pair = remote(half_of(0), half_of(0), plane_send, pair_recv, me, other)
    pair.start()

    for index in range(1, PLANE):
        @pl.when(greets(index))
        def _():
            pl.semaphore_wait(plane_alive.at[index - 1], 1)
            send_plane(index)

    @pl.when((spot == 1) | (spot == 2))
    def _():
        send_plane(3)

    def send_high(step):
        @pl.when(line_peer(step) > me)
        def _():
            pl.semaphore_wait(line_alive.at[step - 1], 2)
            send_row(step)

    small.wait()
    top = jnp.log(jnp.full((1, 1), outscale[0], F32)) * LOG2E
    column = jnp.transpose(jnp.broadcast_to(lengths[...], (feats, feats)))[:, 0:1]

    pair.wait_recv()

    def prepare_columns(index):
        for part in range(2):
            cols = slice(part * share, (part + 1) * share)
            guest = (columns[index, 0, :, cols].astype(F32) / column).astype(BF16)
            wide = guest.astype(F32)
            norm = -0.5 * LOG2E * jnp.sum(wide * wide, axis=0, keepdims=True)
            one = jnp.ones_like(norm)
            stacked = jnp.concatenate(
                [guest, guest, guest, extra_rows(pieces(norm) + (one, one, one))], axis=0)
            right[index, cols, :] = stacked.T

    def prepare_rows(step, value):
        scaled = (value.astype(F32) / column).astype(BF16).astype(F32)
        height = -0.5 * LOG2E * jnp.sum(scaled * scaled, axis=0, keepdims=True) + top
        one = jnp.ones_like(height)
        for index, piece in enumerate(pieces(scaled * LOG2E)):
            left[step, index * feats:(index + 1) * feats, :] = piece.astype(BF16)
        left[step, 3 * feats:, :] = extra_rows((one, one, one) + pieces(height))

    def unit(step, index):
        power = jnp.dot(right[index], left[step], preferred_element_type=F32)
        value = jnp.exp2(jnp.minimum(power, top)).astype(BF16)
        return jnp.dot(columns[index, 1], value, preferred_element_type=F32)

    def give_back(step, feat):
        return remote(part_out.at[step, feat], inbox.at[step, core], part_send, part_recv,
                      line_peer(step), feat)

    def forward(index):
        plane_arrival(index).wait_recv()
        twin(index).start()

    def open_column(index):
        twin(index).wait_recv()
        prepare_columns(index)

    def open_row(step):
        row_arrival(step).wait_recv()
        prepare_rows(step, row_points[step])

    def add_unit(step, index):
        total[step] += unit(step, index)

    def send_back(step):
        for feat in range(2):
            part_out[step, feat] = (
                total[step, feat * half:(feat + 1) * half, :].astype(BF16))
        for feat in range(2):
            give_back(step, feat).start()

    second = jnp.maximum(level, 2)
    prepare_columns(0)

    def first(place):
        step = jnp.where(place == 2, second, place)

        @pl.when(place == 0)
        def _():
            prepare_rows(step, columns[0, 0, :, my_cols])

        @pl.when(place == 1)
        def _():
            loop(1, line, send_high)

        @pl.when(place > 0)
        def _():
            open_row(step)

        total[step] = unit(step, 0)

        for index in range(1, PLANE - 1):
            @pl.when(place == index)
            def _():
                forward(index)

    loop(0, 3, first)

    own = jnp.where(level == 0, 1, 0)

    def rest(place):
        step = level ^ (place + jnp.where(place >= level, 1, 0))
        step = jnp.where(level < 2, place + 1, step)
        step = jnp.where(place < line - 1, step, 0)

        @pl.when((step > 1) & (step != second))
        def _():
            open_row(step)
            total[step] = unit(step, 0)

        def one_column(index):
            @pl.when(place == 0)
            def _():
                open_column(index)

            add_unit(step, index)

            @pl.when((place == 0) & (index == 1))
            def _():
                loop(0, own, lambda _: add_unit(0, 1))
                forward(PLANE - 1)

        loop(jnp.where(place < line - 1, 1, 1 + own), PLANE, one_column)

        @pl.when(place < line - 1)
        def _():
            send_back(step)

    loop(0, line, rest)

    swap_out[...] = total[0, other_rows, :]
    swap = remote(swap_out, swap_in, swap_send, swap_recv, me, other)
    swap.start()
    factor = noise[0]
    mine = columns.at[0, 1, my_rows, :]
    result[:, my_cols] = total[0, my_rows, :] + factor * mine[:, my_cols].astype(F32)
    result[:, other_cols] = factor * mine[:, other_cols].astype(F32)

    whole = columns.at[:, :, my_rows, :]
    remote(whole, whole, plane_send, pair_recv, me, other).wait_send()
    guests = columns.at[1:PLANE, :, my_rows, :]
    remote(guests, guests, twin_send, pair_recv, me, other).wait_send()
    given = row_points.at[1:line]
    remote(given, given, row_send, pair_recv, me, other).wait_send()
    back = remote(part_out.at[1:line], inbox.at[1:line], part_send, part_recv, me, other)
    back.wait_send()
    back.wait_recv()

    def collect(step):
        for feat in range(2):
            result[:, feat * share:(feat + 1) * share] += inbox[step, feat].astype(F32)

    loop(1, line, collect)
    swap.wait_recv()
    result[:, other_cols] += swap_in[...]
    swap.wait_send()


def per_device(blk, points, vectors, lengthscale, outscale, noise):
    assert blk % (4 * PLANE) == 0 and blk & (blk - 1) == 0
    line = blk // PLANE
    rows, half = points.shape
    feats = 2 * half
    share = rows // 2
    stay = pl.BlockSpec(memory_space=pltpu.HBM)
    scalar = pl.BlockSpec(memory_space=pltpu.SMEM)
    vmem = pl.BlockSpec(memory_space=pltpu.VMEM)
    dma = pltpu.SemaphoreType.DMA
    regular = pltpu.SemaphoreType.REGULAR
    wide = 3 * feats + EXTRA
    out = pl.pallas_call(
        functools.partial(kernel, line),
        out_shape=pltpu.VMEM((half, rows), F32),
        in_specs=[stay] * 3 + [scalar] * 2,
        out_specs=vmem,
        scratch_shapes=[
            pltpu.VMEM((1, feats), F32),
            pltpu.VMEM((PLANE, 2, feats, rows), BF16),
            pltpu.VMEM((line, feats, share), BF16),
            pltpu.VMEM((PLANE, rows, wide), BF16),
            pltpu.VMEM((line, wide, share), BF16),
            pltpu.VMEM((line, feats, share), F32),
            pltpu.VMEM((line, 2, half, share), BF16),
            pltpu.VMEM((line, 2, half, share), BF16),
            pltpu.VMEM((half, share), F32),
            pltpu.VMEM((half, share), F32),
            regular,
            regular((PLANE - 1,)),
            regular((line - 1,)),
            dma,
            dma,
            dma,
            dma,
            dma((PLANE - 1,)),
            dma,
            dma((PLANE - 1,)),
            dma,
            dma((line - 1,)),
            dma,
            dma,
            dma,
            dma,
        ],
        compiler_params=pltpu.CompilerParams(collective_id=0, has_side_effects=True),
        name="tile_solve",
    )(points.T, vectors.T, lengthscale.reshape(1, feats), outscale, noise)
    return out.T


def solution(mesh):
    placed = (P("blk", "feat"), P("blk", "feat"), P(), P(), P())
    return jax.shard_map(
        functools.partial(per_device, mesh.shape["blk"]),
        mesh=mesh, in_specs=placed, out_specs=P("blk", "feat"), check_vma=False,
    )
```

time: 24.9 us -> 23.3 us (0.936)
  the two profiles are of different devices: /device:TPU:27 before, /device:TPU:17 now
where the time goes in v3:
time: 23.3 us; the launch traced here: 23.1 us
  Pallas kernels  21.1 us (91%)
  between operations  1.3 us (6%)
  local copies, waits for them, and re-layouts  0.66 us (3%)
    pallas_call x1, Pallas kernels, per_device(): pl.pallas_call(functools.partial(kernel, line), out_shape=pltpu.VMEM((hal...  21.1 us
    unnamed x1, local copies, waits for them, and re-layouts  0.66 us

profile of v3, /device:TPU:17, one launch (start us, length us, event | category | flops | bytes accessed | tf_op | source)
XLA Modules:
  0.0 23.1 jit_solution(5441894196791525305)
XLA Ops:
  1.3 21.1 %tile_solve.1 = f32[32,1024]{1,0:T(8,128)S(1)} custom-call(bf16[32,1024]{1,0:T(8,128)(2,1)} %bitcast.5, bf16[32,1024]{1,0:T(8,128)(2,1)} %bitcast.6, f32[1,64]{1,0:T(1,128)} %bitcast.7, f32[1]{0:T(128)S(6)} %copy.8.outscale, f32[1]{0:T(128)S(6)} %copy.9.noise), custom_call_target="tpu_custom_call" | custom-call | tf_op jit(solution)/shard_map/tile_solve/pallas_call | solution.py:351
  22.4 0.7 %copy.7 = f32[1024,32]{0,1:T(8,128)} copy(f32[1024,32]{0,1:T(8,128)S(1)} %bitcast.4) | data formatting | bytes 262144

commit v4 on v3

--- a/solution.py
+++ b/solution.py
@@ -193,6 +193,7 @@
             pl.semaphore_wait(line_alive.at[step - 1], 2)
             send_row(step)
 
+    loop(1, line, send_high)
     small.wait()
     top = jnp.log(jnp.full((1, 1), outscale[0], F32)) * LOG2E
     column = jnp.transpose(jnp.broadcast_to(lengths[...], (feats, feats)))[:, 0:1]
@@ -223,6 +224,15 @@
         value = jnp.exp2(jnp.minimum(power, top)).astype(BF16)
         return jnp.dot(columns[index, 1], value, preferred_element_type=F32)
 
+    def span(step, start):
+        guests = right[start:].reshape((PLANE - start) * rows, right.shape[2])
+        power = jnp.dot(guests, left[step], preferred_element_type=F32)
+        value = jnp.exp2(jnp.minimum(power, top)).astype(BF16)
+        return sum(
+            jnp.dot(columns[start + place, 1], value[place * rows:(place + 1) * rows],
+                    preferred_element_type=F32)
+            for place in range(PLANE - start))
+
     def give_back(step, feat):
         return remote(part_out.at[step, feat], inbox.at[step, core], part_send, part_recv,
                       line_peer(step), feat)
@@ -259,10 +269,6 @@
         def _():
             prepare_rows(step, columns[0, 0, :, my_cols])
 
-        @pl.when(place == 1)
-        def _():
-            loop(1, line, send_high)
-
         @pl.when(place > 0)
         def _():
             open_row(step)
@@ -280,13 +286,21 @@
 
     def rest(place):
         step = level ^ (place + jnp.where(place >= level, 1, 0))
-        step = jnp.where(level < 2, place + 1, step)
+        step = jnp.where(level == 1, place + 1, step)
+        step = jnp.where(level == 0, jnp.where(place < line - 2, place + 2, 1), step)
         step = jnp.where(place < line - 1, step, 0)
 
-        @pl.when((step > 1) & (step != second))
+        fresh = (step > 1) & (step != second)
+        alone = (place == 0) | ((place == line - 1) & (level == 0))
+
+        @pl.when(fresh)
         def _():
             open_row(step)
-            total[step] = unit(step, 0)
+            total[step] = span(step, 0)
+
+        @pl.when(jnp.logical_not(fresh | alone))
+        def _():
+            total[step] += span(step, 1)
 
         def one_column(index):
             @pl.when(place == 0)
@@ -300,7 +314,7 @@
                 loop(0, own, lambda _: add_unit(0, 1))
                 forward(PLANE - 1)
 
-        loop(jnp.where(place < line - 1, 1, 1 + own), PLANE, one_column)
+        loop(jnp.where(alone, jnp.where(place == 0, 1, 2), PLANE), PLANE, one_column)
 
         @pl.when(place < line - 1)
         def _():

time: 23.3 us -> 22.7 us (0.974)
  the two profiles are of different devices: /device:TPU:17 before, /device:TPU:13 now
where the time goes in v4:
time: 22.7 us; the launch traced here: 22.4 us
  Pallas kernels  20.4 us (90%)
  between operations  1.3 us (6%)
  local copies, waits for them, and re-layouts  0.66 us (3%)
    pallas_call x1, Pallas kernels, per_device(): pl.pallas_call(functools.partial(kernel, line), out_shape=pltpu.VMEM((hal...  20.4 us
    unnamed x1, local copies, waits for them, and re-layouts  0.66 us

profile of v4, /device:TPU:13, one launch (start us, length us, event | category | flops | bytes accessed | tf_op | source)
XLA Modules:
  0.0 22.4 jit_solution(6474012453530301629)
XLA Ops:
  1.3 20.4 %tile_solve.1 = f32[32,1024]{1,0:T(8,128)S(1)} custom-call(bf16[32,1024]{1,0:T(8,128)(2,1)} %bitcast.5, bf16[32,1024]{1,0:T(8,128)(2,1)} %bitcast.6, f32[1,64]{1,0:T(1,128)} %bitcast.7, f32[1]{0:T(128)S(6)} %copy.8.outscale, f32[1]{0:T(128)S(6)} %copy.9.noise), custom_call_target="tpu_custom_call" | custom-call | tf_op jit(solution)/shard_map/tile_solve/pallas_call | solution.py:365
  21.7 0.7 %copy.7 = f32[1024,32]{0,1:T(8,128)} copy(f32[1024,32]{0,1:T(8,128)S(1)} %bitcast.4) | data formatting | bytes 262144

commit v5 on v4

--- a/solution.py
+++ b/solution.py
@@ -32,7 +32,7 @@
 
 def kernel(
     line, points, vectors, lengths_in, outscale, noise, result,
-    lengths, columns, row_points, right, left, total, part_out, inbox, swap_out, swap_in,
+    lengths, columns, row_points, right, left, total, held, part_out, inbox, swap_out, swap_in,
     twin_alive, plane_alive, line_alive,
     small_sem, local_sem, plane_send, pair_recv, plane_recv, twin_send, twin_recv,
     row_send, row_recv, part_send, part_recv, swap_send, swap_recv,
@@ -134,18 +134,31 @@
     def half_of(index):
         return columns.at[index, :, my_rows, :]
 
+    def slot(index, kind):
+        return PLANE - 1 if kind == 1 and index == PLANE - 1 else index - 1
+
+    def part_of(index, kind):
+        return half_of(index) if kind is None else columns.at[index, kind, my_rows, :]
+
     def send_plane(index):
+        target = index
+        if index > 1:
+            target = jnp.where(spot ^ index == 2, 5 - index, index)
         for kind, array in enumerate(inputs):
-            remote(array, columns.at[index, kind, my_rows, :], plane_send,
-                   plane_recv.at[index - 1], plane_peer(index), core).start()
-
-    def plane_arrival(index):
-        return remote(half_of(index), half_of(index), plane_send, plane_recv.at[index - 1],
+            arrive = target - 1
+            if index > 1 and kind == 1:
+                arrive = jnp.where(target == PLANE - 1, PLANE - 1, target - 1)
+            remote(array, columns.at[target, kind, my_rows, :], plane_send,
+                   plane_recv.at[arrive], plane_peer(index), core).start()
+
+    def plane_arrival(index, kind=None):
+        place = part_of(index, kind)
+        return remote(place, place, plane_send, plane_recv.at[slot(index, kind)],
                       plane_peer(index), core)
 
-    def twin(index):
-        return remote(half_of(index), half_of(index), twin_send, twin_recv.at[index - 1],
-                      me, other)
+    def twin(index, kind=None):
+        place = part_of(index, kind)
+        return remote(place, place, twin_send, twin_recv.at[slot(index, kind)], me, other)
 
     def send_row(step):
         for feat in range(2):
@@ -219,10 +232,12 @@
             left[step, index * feats:(index + 1) * feats, :] = piece.astype(BF16)
         left[step, 3 * feats:, :] = extra_rows((one, one, one) + pieces(height))
 
+    def entries(step, index):
+        power = jnp.dot(right[index], left[step], preferred_element_type=F32)
+        return jnp.exp2(jnp.minimum(power, top)).astype(BF16)
+
     def unit(step, index):
-        power = jnp.dot(right[index], left[step], preferred_element_type=F32)
-        value = jnp.exp2(jnp.minimum(power, top)).astype(BF16)
-        return jnp.dot(columns[index, 1], value, preferred_element_type=F32)
+        return jnp.dot(columns[index, 1], entries(step, index), preferred_element_type=F32)
 
     def span(step, start):
         guests = right[start:].reshape((PLANE - start) * rows, right.shape[2])
@@ -237,12 +252,12 @@
         return remote(part_out.at[step, feat], inbox.at[step, core], part_send, part_recv,
                       line_peer(step), feat)
 
-    def forward(index):
-        plane_arrival(index).wait_recv()
-        twin(index).start()
-
-    def open_column(index):
-        twin(index).wait_recv()
+    def forward(index, kind=None):
+        plane_arrival(index, kind).wait_recv()
+        twin(index, kind).start()
+
+    def open_column(index, kind=None):
+        twin(index, kind).wait_recv()
         prepare_columns(index)
 
     def open_row(step):
@@ -283,6 +298,7 @@
     loop(0, 3, first)
 
     own = jnp.where(level == 0, 1, 0)
+    soon = (core == 1) | (spot == 2)
 
     def rest(place):
         step = level ^ (place + jnp.where(place >= level, 1, 0))
@@ -303,7 +319,7 @@
             total[step] += span(step, 1)
 
         def one_column(index):
-            @pl.when(place == 0)
+            @pl.when((place == 0) & (index < PLANE - 1))
             def _():
                 open_column(index)
 
@@ -312,9 +328,22 @@
             @pl.when((place == 0) & (index == 1))
             def _():
                 loop(0, own, lambda _: add_unit(0, 1))
-                forward(PLANE - 1)
-
-        loop(jnp.where(alone, jnp.where(place == 0, 1, 2), PLANE), PLANE, one_column)
+                forward(PLANE - 1, 0)
+
+            @pl.when((place == 0) & (index == jnp.where(soon, 1, PLANE - 2)))
+            def _():
+                forward(PLANE - 1, 1)
+
+        loop(jnp.where(alone, jnp.where(place == 0, 1, 2), PLANE),
+             jnp.where(place == 0, PLANE - 1, PLANE), one_column)
+
+        @pl.when(place == 0)
+        def _():
+            open_column(PLANE - 1, 0)
+            held[...] = entries(step, PLANE - 1)
+            twin(PLANE - 1, 1).wait_recv()
+            total[step] += jnp.dot(columns[PLANE - 1, 1], held[...],
+                                   preferred_element_type=F32)
 
         @pl.when(place < line - 1)
         def _():
@@ -374,6 +403,7 @@
             pltpu.VMEM((PLANE, rows, wide), BF16),
             pltpu.VMEM((line, wide, share), BF16),
             pltpu.VMEM((line, feats, share), F32),
+            pltpu.VMEM((rows, share), BF16),
             pltpu.VMEM((line, 2, half, share), BF16),
             pltpu.VMEM((line, 2, half, share), BF16),
             pltpu.VMEM((half, share), F32),
@@ -385,9 +415,9 @@
             dma,
             dma,
             dma,
-            dma((PLANE - 1,)),
-            dma,
-            dma((PLANE - 1,)),
+            dma((PLANE,)),
+            dma,
+            dma((PLANE,)),
             dma,
             dma((line - 1,)),
             dma,

time: 22.7 us -> 22.4 us (0.987)
  no operation moved by 1% of the time
where the time goes in v5:
time: 22.4 us; the launch traced here: 22.2 us
  Pallas kernels  20.2 us (90%)
  between operations  1.3 us (6%)
  local copies, waits for them, and re-layouts  0.66 us (3%)
    pallas_call x1, Pallas kernels, per_device(): pl.pallas_call(functools.partial(kernel, line), out_shape=pltpu.VMEM((hal...  20.2 us
    unnamed x1, local copies, waits for them, and re-layouts  0.66 us

profile of v5, /device:TPU:13, one launch (start us, length us, event | category | flops | bytes accessed | tf_op | source)
XLA Modules:
  0.0 22.2 jit_solution(1507507193263289889)
XLA Ops:
  1.3 20.2 %tile_solve.1 = f32[32,1024]{1,0:T(8,128)S(1)} custom-call(bf16[32,1024]{1,0:T(8,128)(2,1)} %bitcast.5, bf16[32,1024]{1,0:T(8,128)(2,1)} %bitcast.6, f32[1,64]{1,0:T(1,128)} %bitcast.7, f32[1]{0:T(128)S(6)} %copy.8.outscale, f32[1]{0:T(128)S(6)} %copy.9.noise), custom_call_target="tpu_custom_call" | custom-call | tf_op jit(solution)/shard_map/tile_solve/pallas_call | solution.py:394
  21.5 0.7 %copy.7 = f32[1024,32]{0,1:T(8,128)} copy(f32[1024,32]{0,1:T(8,128)S(1)} %bitcast.4) | data formatting | bytes 262144

commit v6 on v5

--- a/solution.py
+++ b/solution.py
@@ -138,18 +138,19 @@
         return PLANE - 1 if kind == 1 and index == PLANE - 1 else index - 1
 
     def part_of(index, kind):
-        return half_of(index) if kind is None else columns.at[index, kind, my_rows, :]
+        if kind is None:
+            return half_of(index)
+        return columns.at[index, kind, :, my_cols]
 
     def send_plane(index):
-        target = index
-        if index > 1:
-            target = jnp.where(spot ^ index == 2, 5 - index, index)
         for kind, array in enumerate(inputs):
-            arrive = target - 1
-            if index > 1 and kind == 1:
-                arrive = jnp.where(target == PLANE - 1, PLANE - 1, target - 1)
-            remote(array, columns.at[target, kind, my_rows, :], plane_send,
-                   plane_recv.at[arrive], plane_peer(index), core).start()
+            remote(array, columns.at[index, kind, my_rows, :], plane_send,
+                   plane_recv.at[index - 1], plane_peer(index), core).start()
+
+    def send_last():
+        for kind in range(2):
+            remote(part_of(0, kind), part_of(PLANE - 1, kind), plane_send,
+                   plane_recv.at[slot(PLANE - 1, kind)], plane_peer(PLANE - 1), core).start()
 
     def plane_arrival(index, kind=None):
         place = part_of(index, kind)
@@ -170,7 +171,7 @@
         return remote(row_points.at[step], row_points.at[step], row_send,
                       row_recv.at[step - 1], line_peer(step), core)
 
-    for index in range(1, PLANE):
+    for index in range(1, PLANE - 1):
         @pl.when(answers(index))
         def _():
             send_plane(index)
@@ -190,15 +191,18 @@
     pair = remote(half_of(0), half_of(0), plane_send, pair_recv, me, other)
     pair.start()
 
-    for index in range(1, PLANE):
+    for index in range(1, PLANE - 1):
         @pl.when(greets(index))
         def _():
             pl.semaphore_wait(plane_alive.at[index - 1], 1)
             send_plane(index)
 
-    @pl.when((spot == 1) | (spot == 2))
+    @pl.when(greets(PLANE - 1))
     def _():
-        send_plane(3)
+        pl.semaphore_wait(plane_alive.at[PLANE - 2], 1)
+
+    pair.wait_recv()
+    send_last()
 
     def send_high(step):
         @pl.when(line_peer(step) > me)
@@ -211,11 +215,8 @@
     top = jnp.log(jnp.full((1, 1), outscale[0], F32)) * LOG2E
     column = jnp.transpose(jnp.broadcast_to(lengths[...], (feats, feats)))[:, 0:1]
 
-    pair.wait_recv()
-
-    def prepare_columns(index):
-        for part in range(2):
-            cols = slice(part * share, (part + 1) * share)
+    def prepare_columns(index, parts=(slice(0, share), slice(share, rows))):
+        for cols in parts:
             guest = (columns[index, 0, :, cols].astype(F32) / column).astype(BF16)
             wide = guest.astype(F32)
             norm = -0.5 * LOG2E * jnp.sum(wide * wide, axis=0, keepdims=True)
@@ -232,17 +233,17 @@
             left[step, index * feats:(index + 1) * feats, :] = piece.astype(BF16)
         left[step, 3 * feats:, :] = extra_rows((one, one, one) + pieces(height))
 
-    def entries(step, index):
-        power = jnp.dot(right[index], left[step], preferred_element_type=F32)
+    def entries(step, guests):
+        power = jnp.dot(guests, left[step], preferred_element_type=F32)
         return jnp.exp2(jnp.minimum(power, top)).astype(BF16)
 
     def unit(step, index):
-        return jnp.dot(columns[index, 1], entries(step, index), preferred_element_type=F32)
+        return jnp.dot(columns[index, 1], entries(step, right[index]),
+                       preferred_element_type=F32)
 
     def span(step, start):
         guests = right[start:].reshape((PLANE - start) * rows, right.shape[2])
-        power = jnp.dot(guests, left[step], preferred_element_type=F32)
-        value = jnp.exp2(jnp.minimum(power, top)).astype(BF16)
+        value = entries(step, guests)
         return sum(
             jnp.dot(columns[start + place, 1], value[place * rows:(place + 1) * rows],
                     preferred_element_type=F32)
@@ -256,8 +257,8 @@
         plane_arrival(index, kind).wait_recv()
         twin(index, kind).start()
 
-    def open_column(index, kind=None):
-        twin(index, kind).wait_recv()
+    def open_column(index):
+        twin(index).wait_recv()
         prepare_columns(index)
 
     def open_row(step):
@@ -300,6 +301,14 @@
     own = jnp.where(level == 0, 1, 0)
     soon = (core == 1) | (spot == 2)
 
+    last = PLANE - 1
+
+    def own_half(step):
+        prepare_columns(last, (my_cols,))
+        total[step] += jnp.dot(
+            columns[last, 1, :, my_cols], entries(step, right[last, my_cols, :]),
+            preferred_element_type=F32)
+
     def rest(place):
         step = level ^ (place + jnp.where(place >= level, 1, 0))
         step = jnp.where(level == 1, place + 1, step)
@@ -334,15 +343,24 @@
             def _():
                 forward(PLANE - 1, 1)
 
+            @pl.when(soon & (place == 0) & (index == 1))
+            def _():
+                own_half(step)
+
         loop(jnp.where(alone, jnp.where(place == 0, 1, 2), PLANE),
              jnp.where(place == 0, PLANE - 1, PLANE), one_column)
 
         @pl.when(place == 0)
         def _():
-            open_column(PLANE - 1, 0)
-            held[...] = entries(step, PLANE - 1)
-            twin(PLANE - 1, 1).wait_recv()
-            total[step] += jnp.dot(columns[PLANE - 1, 1], held[...],
+            @pl.when(jnp.logical_not(soon))
+            def _():
+                own_half(step)
+
+            twin(last, 0).wait_recv()
+            prepare_columns(last, (other_cols,))
+            held[...] = entries(step, right[last, other_cols, :])
+            twin(last, 1).wait_recv()
+            total[step] += jnp.dot(columns[last, 1, :, other_cols], held[...],
                                    preferred_element_type=F32)
 
         @pl.when(place < line - 1)
@@ -403,7 +421,7 @@
             pltpu.VMEM((PLANE, rows, wide), BF16),
             pltpu.VMEM((line, wide, share), BF16),
             pltpu.VMEM((line, feats, share), F32),
-            pltpu.VMEM((rows, share), BF16),
+            pltpu.VMEM((share, share), BF16),
             pltpu.VMEM((line, 2, half, share), BF16),
             pltpu.VMEM((line, 2, half, share), BF16),
             pltpu.VMEM((half, share), F32),

time: 22.4 us -> 22.3 us (level)
  no operation moved by 1% of the time
where the time goes in v6:
time: 22.3 us; the launch traced here: 22.2 us
  Pallas kernels  20.2 us (91%)
  between operations  1.3 us (6%)
  local copies, waits for them, and re-layouts  0.66 us (3%)
    pallas_call x1, Pallas kernels, per_device(): pl.pallas_call(functools.partial(kernel, line), out_shape=pltpu.VMEM((hal...  20.2 us
    unnamed x1, local copies, waits for them, and re-layouts  0.66 us

profile of v6, /device:TPU:13, one launch (start us, length us, event | category | flops | bytes accessed | tf_op | source)
XLA Modules:
  0.0 22.2 jit_solution(15260277406868853927)
XLA Ops:
  1.3 20.2 %tile_solve.1 = f32[32,1024]{1,0:T(8,128)S(1)} custom-call(bf16[32,1024]{1,0:T(8,128)(2,1)} %bitcast.5, bf16[32,1024]{1,0:T(8,128)(2,1)} %bitcast.6, f32[1,64]{1,0:T(1,128)} %bitcast.7, f32[1]{0:T(128)S(6)} %copy.8.outscale, f32[1]{0:T(128)S(6)} %copy.9.noise), custom_call_target="tpu_custom_call" | custom-call | tf_op jit(solution)/shard_map/tile_solve/pallas_call | solution.py:412
  21.5 0.7 %copy.7 = f32[1024,32]{0,1:T(8,128)} copy(f32[1024,32]{0,1:T(8,128)S(1)} %bitcast.4) | data formatting | bytes 262144

commit v7 on v5

--- a/solution.py
+++ b/solution.py
@@ -140,7 +140,7 @@
     def part_of(index, kind):
         return half_of(index) if kind is None else columns.at[index, kind, my_rows, :]
 
-    def send_plane(index):
+    def send_plane(index, kept=True):
         target = index
         if index > 1:
             target = jnp.where(spot ^ index == 2, 5 - index, index)
@@ -148,7 +148,8 @@
             arrive = target - 1
             if index > 1 and kind == 1:
                 arrive = jnp.where(target == PLANE - 1, PLANE - 1, target - 1)
-            remote(array, columns.at[target, kind, my_rows, :], plane_send,
+            source = columns.at[0, kind, my_rows, :] if kept else array
+            remote(source, columns.at[target, kind, my_rows, :], plane_send,
                    plane_recv.at[arrive], plane_peer(index), core).start()
 
     def plane_arrival(index, kind=None):
@@ -170,6 +171,7 @@
         return remote(row_points.at[step], row_points.at[step], row_send,
                       row_recv.at[step - 1], line_peer(step), core)
 
+    pltpu.make_async_copy(half_of(0), half_of(0), local_sem).wait()
     for index in range(1, PLANE):
         @pl.when(answers(index))
         def _():
@@ -180,7 +182,6 @@
         def _():
             send_row(step)
 
-    pltpu.make_async_copy(half_of(0), half_of(0), local_sem).wait()
     loop(1, line, send_low)
 
     @pl.when(core == 0)

time: 22.4 us -> 22.2 us (level)
  no operation moved by 1% of the time
where the time goes in v7:
time: 22.2 us; the launch traced here: 22 us
  Pallas kernels  20.1 us (91%)
  between operations  1.3 us (6%)
  local copies, waits for them, and re-layouts  0.66 us (3%)
    pallas_call x1, Pallas kernels, per_device(): pl.pallas_call(functools.partial(kernel, line), out_shape=pltpu.VMEM((hal...  20.1 us
    unnamed x1, local copies, waits for them, and re-layouts  0.66 us

profile of v7, /device:TPU:13, one launch (start us, length us, event | category | flops | bytes accessed | tf_op | source)
XLA Modules:
  0.0 22.0 jit_solution(5717586253967098374)
XLA Ops:
  1.3 20.1 %tile_solve.1 = f32[32,1024]{1,0:T(8,128)S(1)} custom-call(bf16[32,1024]{1,0:T(8,128)(2,1)} %bitcast.5, bf16[32,1024]{1,0:T(8,128)(2,1)} %bitcast.6, f32[1,64]{1,0:T(1,128)} %bitcast.7, f32[1]{0:T(128)S(6)} %copy.8.outscale, f32[1]{0:T(128)S(6)} %copy.9.noise), custom_call_target="tpu_custom_call" | custom-call | tf_op jit(solution)/shard_map/tile_solve/pallas_call | solution.py:395
  21.4 0.7 %copy.7 = f32[1024,32]{0,1:T(8,128)} copy(f32[1024,32]{0,1:T(8,128)S(1)} %bitcast.4) | data formatting | bytes 262144
